TPU v7x, 32 devices: a whole 2x2x4 slice. The times are simulated.
32 devices in a mesh: parts: 2 (over y), gz: 4 (over x, core), ty: 4 (over z).
Axes of the slice: x: 2, y: 2, z: 4, core: 2. Of those that a mesh axis runs over, the one named last changes fastest.
Arguments:
- sections: bfloat16 [8, 1024, 2048], P(('parts', 'gz'), 'ty'), parts along dimension 0, may hold values from -6 to 6
- boundary: bfloat16 [2048, 2048], P(('parts', 'ty')), parts along dimension 0, may hold values from -5 to 5
- row_shift: int32 [8, 1024], P(('parts', 'gz'), 'ty'), parts along dimension 0, may hold values from -64 to 63
- row_frac: int32 [8, 1024], P(('parts', 'gz'), 'ty'), parts along dimension 0, may hold values from 0 to 255
- col_shift: int32 [8, 2048], P(('parts', 'gz')), parts along dimension 0, may hold values from -64 to 63
- col_frac: int32 [8, 2048], P(('parts', 'gz')), parts along dimension 0, may hold values from 0 to 255
- peak_shift: int32 [2, 8, 8, 16], P(None, ('parts', 'gz'), 'ty'), parts along dimension 1, may hold values from -8 to 8
Outputs:
- rendered: bfloat16 [8, 1024, 2048], P(('parts', 'gz'), 'ty'), parts along dimension 0
- flow: float32 [2, 8, 8, 16], P(None, ('parts', 'gz'), 'ty'), parts along dimension 1
There are 2 independent parts, one for each index of `parts`. A program takes and returns all parts, laid end to end along the dimension named above; each array names one. Nothing has to cross between parts.
All inputs are finite; a program needn't handle non-finite values.
Results may differ from a plain program's by a relative error of at most 0.0049.
Values may be sent and summed in bfloat16 or wider, within the bound.
A program may use at most 64 MiB of HBM per device.

v0:
```python
import functools

import jax
import jax.numpy as jnp
import numpy as np
from jax import lax
from jax.experimental import pallas as pl
from jax.experimental.pallas import tpu as pltpu
from jax.sharding import PartitionSpec as P

PATCH = 128
MARGIN = 64
SMOOTH_PASSES = 2
TAPS = (0.0625, 0.25, 0.375, 0.25, 0.0625)
BLOCK = 256


def smooth_operator(n):
    kernel = np.zeros((n, n))
    for k, tap in enumerate(TAPS):
        kernel += tap * np.eye(n, k=k - 2)
    kernel = kernel / kernel.sum(axis=1, keepdims=True)
    return np.linalg.matrix_power(kernel, SMOOTH_PASSES)


def two_tap(ids, first, weight):
    d = ids - first
    return jnp.where(d == 0, 1.0 - weight, jnp.where(d == 1, weight, 0.0)).astype(jnp.bfloat16)


def render_kernel(all_rows, sec, above, below, rshift, rfrac, cshift, cfrac, out, stack, mix):
    n_rows, n_cols = sec.shape
    tile = lax.axis_index("ty")
    stack[0:MARGIN] = above[...]
    stack[MARGIN : MARGIN + n_rows] = sec[...]
    stack[MARGIN + n_rows :] = below[...]
    span = PATCH + 2 * MARGIN
    for p in range(n_rows // PATCH):
        at = p * PATCH
        y = tile * n_rows + at + lax.broadcasted_iota(jnp.int32, (1, PATCH), 1)
        src = jnp.clip(y + rshift[:, at : at + PATCH], 0, all_rows - 2)
        src = src - (tile * n_rows - MARGIN + at)
        weight = rfrac[:, at : at + PATCH].astype(jnp.float32) / 256.0
        ids = lax.broadcasted_iota(jnp.int32, (span, PATCH), 0)
        table = two_tap(ids, src, weight)
        mix[at : at + PATCH] = lax.dot_general(
            table,
            stack[at : at + span],
            (((0,), (0,)), ((), ())),
            preferred_element_type=jnp.float32,
        ).astype(jnp.bfloat16)
    for x0 in range(0, n_cols, BLOCK):
        lo, hi = max(x0 - PATCH, 0), min(x0 + BLOCK + PATCH, n_cols)
        x = x0 + lax.broadcasted_iota(jnp.int32, (1, BLOCK), 1)
        src = jnp.clip(x + cshift[:, x0 : x0 + BLOCK], 0, n_cols - 2) - lo
        weight = cfrac[:, x0 : x0 + BLOCK].astype(jnp.float32) / 256.0
        ids = lax.broadcasted_iota(jnp.int32, (hi - lo, BLOCK), 0)
        table = two_tap(ids, src, weight)
        out[:, x0 : x0 + BLOCK] = jnp.dot(
            mix[:, lo:hi], table, preferred_element_type=jnp.float32
        ).astype(jnp.bfloat16)


def patch_sums(a, b, py, px):
    a = a.astype(jnp.float32)
    b = b.astype(jnp.float32)
    b = pltpu.roll(b, (PATCH - px) % PATCH, 1)
    b = pltpu.roll(b, (PATCH - py) % PATCH, 0)
    bs = (pltpu.roll(b, 1, 0), b, pltpu.roll(b, PATCH - 1, 0))
    sums = []
    as_ = (pltpu.roll(a, PATCH - 1, 1), a, pltpu.roll(a, 1, 1))
    for dy in range(3):
        for dx in range(3):
            sums.append(jnp.sum(as_[dx] * bs[dy], axis=0, keepdims=True))
    return sums


def flow_from(acc, peaks):
    w = [jnp.maximum(jnp.sum(acc[k], axis=-1, keepdims=True) / PATCH, 0.0) for k in range(9)]
    total = jnp.maximum(functools.reduce(lambda p, q: p + q, w), 1.0)
    row = (w[6] + w[7] + w[8]) - (w[0] + w[1] + w[2])
    col = (w[2] + w[5] + w[8]) - (w[0] + w[3] + w[6])
    return peaks[0] + row / total, peaks[1] + col / total


def window_kernel(peak, cur, shifted, boundary, out, old, acc, peaks, sem):
    n_rows, n_cols = cur.shape
    n_px = n_cols // PATCH
    first = lax.axis_index("gz") == 0

    @pl.when(first)
    def _():
        pltpu.make_async_copy(boundary, old, sem).start()

    @pl.when(jnp.logical_not(first))
    def _():
        pltpu.make_async_copy(shifted, old, sem).start()

    pltpu.make_async_copy(shifted, old, sem).wait()

    def column(j, carry):
        cols = pl.ds(pl.multiple_of(j * PATCH, PATCH), PATCH)
        for p in range(n_rows // PATCH):
            rows = slice(p * PATCH, (p + 1) * PATCH)
            py, px = peak[0, p * n_px + j], peak[1, p * n_px + j]
            sums = patch_sums(cur[rows, cols], old[rows, cols], py, px)
            at = pl.ds(p * n_px + j, 1)
            for k in range(9):
                acc[k, at, :] = sums[k]
            peaks[0, at, :] = jnp.full((1, PATCH), py, jnp.int32).astype(jnp.float32)
            peaks[1, at, :] = jnp.full((1, PATCH), px, jnp.int32).astype(jnp.float32)
        return carry

    lax.fori_loop(0, n_px, column, 0)
    row, col = flow_from(acc, peaks)
    out[0] = row
    out[1] = col


def shift(x, axis, by):
    peers = lax.axis_size(axis)
    pairs = [(i, i + by) for i in range(peers) if 0 <= i + by < peers]
    return lax.ppermute(x, axis, pairs)


def local(sections, boundary, row_shift, row_frac, col_shift, col_frac, peak_shift):
    n_rows, n_cols = sections.shape[1:]
    tile = lax.axis_index("ty")
    tiles = lax.axis_size("ty")
    sec = sections[0]
    above = shift(sec[n_rows - MARGIN :], "ty", 1)
    below = shift(sec[:MARGIN], "ty", -1)
    rendered = pl.pallas_call(
        functools.partial(render_kernel, n_rows * tiles),
        out_shape=jax.ShapeDtypeStruct((n_rows, n_cols), jnp.bfloat16),
        scratch_shapes=[
            pltpu.VMEM((n_rows + 2 * MARGIN, n_cols), jnp.bfloat16),
            pltpu.VMEM((n_rows, n_cols), jnp.bfloat16),
        ],
    )(sec, above, below, row_shift, row_frac, col_shift, col_frac)
    shifted = shift(rendered, "gz", 1)
    patch_rows, patch_cols = n_rows // PATCH, n_cols // PATCH
    n_patches = patch_rows * patch_cols
    any_spec = pl.BlockSpec(memory_space=pl.ANY)
    vmem_spec = pl.BlockSpec(memory_space=pltpu.VMEM)
    raw = pl.pallas_call(
        window_kernel,
        out_shape=jax.ShapeDtypeStruct((2, n_patches, PATCH), jnp.float32),
        in_specs=[pl.BlockSpec(memory_space=pltpu.SMEM), vmem_spec, any_spec, any_spec],
        out_specs=vmem_spec,
        scratch_shapes=[
            pltpu.VMEM((n_rows, n_cols), jnp.bfloat16),
            pltpu.VMEM((9, n_patches, PATCH), jnp.float32),
            pltpu.VMEM((2, n_patches, PATCH), jnp.float32),
            pltpu.SemaphoreType.DMA,
        ],
    )(peak_shift.reshape(2, n_patches), rendered, shifted, boundary)
    raw = raw[:, :, 0].reshape(2, patch_rows, patch_cols)
    reach = 2 * SMOOTH_PASSES
    hops = -(-reach // patch_rows)
    parts = [shift(raw, "ty", h) if h else raw for h in range(hops, -hops - 1, -1)]
    field = jnp.concatenate(parts, axis=1)
    width = field.shape[1]
    pad = hops * patch_rows
    rows_op = np.pad(smooth_operator(patch_rows * tiles), ((0, 0), (pad, pad))).astype(np.float32)
    at = tile * patch_rows
    rows_op = lax.dynamic_slice(jnp.asarray(rows_op), (at, at), (patch_rows, width))
    cols_op = jnp.asarray(smooth_operator(patch_cols).astype(np.float32))
    flow = jnp.einsum("yr,crx->cyx", rows_op, field, precision=lax.Precision.HIGHEST)
    flow = jnp.einsum("cyr,xr->cyx", flow, cols_op, precision=lax.Precision.HIGHEST)
    return rendered[None], flow[:, None]


def solution(mesh):
    in_specs = (
        P(("parts", "gz"), "ty", None),
        P(("parts", "ty"), None),
        P(("parts", "gz"), "ty"),
        P(("parts", "gz"), "ty"),
        P(("parts", "gz"), None),
        P(("parts", "gz"), None),
        P(None, ("parts", "gz"), "ty", None),
    )
    out_specs = (P(("parts", "gz"), "ty", None), P(None, ("parts", "gz"), "ty", None))
    return jax.shard_map(local, mesh=mesh, in_specs=in_specs, out_specs=out_specs, check_vma=False)
```

profile of v0, /device:TPU:10, one launch (start us, length us, event | category | flops | bytes accessed | tf_op | source)
XLA Modules:
  0.0 60.9 jit_solution(11669406698063203505)
XLA Ops:
  0.6 1.1 %slice_bitcast_fusion = (bf16[64,2048]{1,0:T(8,128)(2,1)S(1)}, bf16[64,2048]{1,0:T(8,128)(2,1)S(1)}) fusion(bf16[1,256,2048]{2,1,0:T(8,128)(2,1)} %param.9), kind=kLoop, calls=%fused_computation.2 | loop fusion | bytes 1048576 | tf_op jit(solution)/shard_map/slice | solution.py:132
  1.7 3.5 %collective-permute-start = (bf16[64,2048]{1,0:T(8,128)(2,1)S(1)}, bf16[64,2048]{1,0:T(8,128)(2,1)S(1)}, u32[]{:S(2)}, u32[]{:S(2)}) collective-permute-start(bf16[64,2048]{1,0:T(8,128)(2,1)S(1)} %get-tuple-element.7), channel_id=1, source_target_pairs={{0,1},{1,2},{2,3},{4,5},{5,6},{6,7},{8,9},{9,10},{10,11},{12,13},{... | collective-permute-start | bytes 786440 | tf_op jit(solution)/shard_map/ppermute | solution.py:123
  5.2 2.4 %collective-permute-start.1 = (bf16[64,2048]{1,0:T(8,128)(2,1)S(1)}, bf16[64,2048]{1,0:T(8,128)(2,1)S(1)}, u32[]{:S(2)}, u32[]{:S(2)}) collective-permute-start(bf16[64,2048]{1,0:T(8,128)(2,1)S(1)} %get-tuple-element.6), channel_id=1, source_target_pairs={{1,0},{2,1},{3,2},{5,4},{6,5},{7,6},{9,8},{10,9},{11,10},{13,12},{... | collective-permute-start | bytes 786440 | tf_op jit(solution)/shard_map/ppermute | solution.py:123
  7.6 4.1 %collective-permute-done.above = bf16[64,2048]{1,0:T(8,128)(2,1)S(1)} collective-permute-done((bf16[64,2048]{1,0:T(8,128)(2,1)S(1)}, bf16[64,2048]{1,0:T(8,128)(2,1)S(1)}, u32[]{:S(2)}, u32[]{:S(2)}) %collective-permute-start) | collective-permute-done | bytes 262176 | tf_op jit(solution)/shard_map/ppermute | solution.py:123
  11.6 0.0 copy-start.1
  11.6 3.2 %collective-permute-done.1.below = bf16[64,2048]{1,0:T(8,128)(2,1)S(1)} collective-permute-done((bf16[64,2048]{1,0:T(8,128)(2,1)S(1)}, bf16[64,2048]{1,0:T(8,128)(2,1)S(1)}, u32[]{:S(2)}, u32[]{:S(2)}) %collective-permute-start.1) | collective-permute-done | bytes 262176 | tf_op jit(solution)/shard_map/ppermute | solution.py:123
  14.9 0.0 copy-start.2
  14.9 0.0 copy-done.1
  14.9 0.7 %copy-done.2 = bf16[64,2048]{1,0:T(8,128)(2,1)} copy-done((bf16[64,2048]{1,0:T(8,128)(2,1)}, bf16[64,2048]{1,0:T(8,128)(2,1)S(1)}, u32[]{:S(2)}) %copy-start.2) | copy-done | bytes 262168
  15.6 0.0 copy-start.4
  15.6 3.8 %shard_map.104.cur = bf16[256,2048]{1,0:T(8,128)(2,1)} custom-call(bf16[256,2048]{1,0:T(8,128)(2,1)} %bitcast.20, bf16[64,2048]{1,0:T(8,128)(2,1)} %copy-done.1, bf16[64,2048]{1,0:T(8,128)(2,1)} %copy-done.2, s32[1,256]{1,0:T(1,128)} %rshift.1, s32[1,256]{1,0:T(1,128)} %rfrac.1, s32[1,2048]{1,0:T(1,128)} %cshift.1, s32[1,2048]{1,0:T(1,128)} %cfrac.1), custom_call_target="tpu_custom_call" | custom-call | tf_op jit(solution)/shard_map/pallas_call | solution.py:133
  19.4 1.9 %collective-permute-start.2 = (bf16[256,2048]{1,0:T(8,128)(2,1)}, bf16[256,2048]{1,0:T(8,128)(2,1)S(1)}, u32[]{:S(2)}, u32[]{:S(2)}) collective-permute-start(bf16[256,2048]{1,0:T(8,128)(2,1)} %shard_map.104.cur), channel_id=1, source_target_pairs={{0,4},{4,8},{8,12},{1,5},{5,9},{9,13},{2,6},{6,10},{10,14},{3,7},{... | collective-permute-start | bytes 3145736 | tf_op jit(solution)/shard_map/ppermute | solution.py:123
  21.3 0.0 copy-done.4
  21.3 0.6 %reshape.9.peak = s32[2,32]{1,0:T(2,128)} reshape(s32[2,1,2,16]{3,2,1,0:T(2,128)S(1)} %copy-done.4) | data formatting | bytes 512 | tf_op jit(solution)/shard_map/reshape | solution.py:157
  21.9 13.7 %collective-permute-done.2.shifted = bf16[256,2048]{1,0:T(8,128)(2,1)S(1)} collective-permute-done((bf16[256,2048]{1,0:T(8,128)(2,1)}, bf16[256,2048]{1,0:T(8,128)(2,1)S(1)}, u32[]{:S(2)}, u32[]{:S(2)}) %collective-permute-start.2) | collective-permute-done | bytes 1048608 | tf_op jit(solution)/shard_map/ppermute | solution.py:123
  35.7 0.0 copy-start
  35.7 1.0 %copy-done = bf16[256,2048]{1,0:T(8,128)(2,1)} copy-done((bf16[256,2048]{1,0:T(8,128)(2,1)}, bf16[256,2048]{1,0:T(8,128)(2,1)S(1)}, u32[]{:S(2)}) %copy-start) | copy-done | bytes 1048600
  36.7 6.9 %shard_map.105 = f32[2,32,128]{2,1,0:T(8,128)} custom-call(s32[2,32]{1,0:T(2,128)} %reshape.9.peak, bf16[256,2048]{1,0:T(8,128)(2,1)} %shard_map.104.cur, bf16[256,2048]{1,0:T(8,128)(2,1)} %copy-done, bf16[256,2048]{1,0:T(8,128)(2,1)} %boundary.1), custom_call_target="tpu_custom_call" | custom-call | tf_op jit(solution)/shard_map/pallas_call | solution.py:146
  43.6 0.8 %slice_reduce_fusion = f32[2,32]{1,0:T(2,128)S(1)} fusion(f32[2,32,128]{2,1,0:T(8,128)} %shard_map.105), kind=kLoop, calls=%fused_computation.4 | loop fusion | bytes 512 | tf_op jit(solution)/shard_map/slice | solution.py:158
  44.4 0.1 reshape_squeeze.3
  44.5 2.5 %collective-permute-start.3 = (f32[2,2,16]{2,1,0:T(2,128)S(1)}, f32[2,2,16]{2,1,0:T(2,128)S(1)}, u32[]{:S(2)}, u32[]{:S(2)}) collective-permute-start(f32[2,2,16]{2,1,0:T(2,128)S(1)} %reshape_squeeze.3), channel_id=1, source_target_pairs={{0,2},{1,3},{4,6},{5,7},{8,10},{9,11},{12,14},{13,15},{16,18},{17,... | collective-permute-start | bytes 776 | tf_op jit(solution)/shard_map/ppermute | solution.py:123
  47.0 2.3 %collective-permute-start.4 = (f32[2,2,16]{2,1,0:T(2,128)S(1)}, f32[2,2,16]{2,1,0:T(2,128)S(1)}, u32[]{:S(2)}, u32[]{:S(2)}) collective-permute-start(f32[2,2,16]{2,1,0:T(2,128)S(1)} %reshape_squeeze.3), channel_id=1, source_target_pairs={{0,1},{1,2},{2,3},{4,5},{5,6},{6,7},{8,9},{9,10},{10,11},{12,13},{... | collective-permute-start | bytes 776 | tf_op jit(solution)/shard_map/ppermute | solution.py:123
  49.3 3.5 %collective-permute-start.5 = (f32[2,2,16]{2,1,0:T(2,128)S(1)}, f32[2,2,16]{2,1,0:T(2,128)S(1)}, u32[]{:S(2)}, u32[]{:S(2)}) collective-permute-start(f32[2,2,16]{2,1,0:T(2,128)S(1)} %reshape_squeeze.3), channel_id=1, source_target_pairs={{1,0},{2,1},{3,2},{5,4},{6,5},{7,6},{9,8},{10,9},{11,10},{13,12},{... | collective-permute-start | bytes 776 | tf_op jit(solution)/shard_map/ppermute | solution.py:123
  52.8 1.3 %collective-permute-start.6 = (f32[2,2,16]{2,1,0:T(2,128)S(1)}, f32[2,2,16]{2,1,0:T(2,128)S(1)}, u32[]{:S(2)}, u32[]{:S(2)}) collective-permute-start(f32[2,2,16]{2,1,0:T(2,128)S(1)} %reshape_squeeze.3), channel_id=1, source_target_pairs={{2,0},{3,1},{6,4},{7,5},{10,8},{11,9},{14,12},{15,13},{18,16},{19,... | collective-permute-start | bytes 776 | tf_op jit(solution)/shard_map/ppermute | solution.py:123
  54.1 0.0 collective-permute-done.3
  54.1 0.0 collective-permute-done.4
  54.2 0.6 %collective-permute-done.5 = f32[2,2,16]{2,1,0:T(2,128)S(1)} collective-permute-done((f32[2,2,16]{2,1,0:T(2,128)S(1)}, f32[2,2,16]{2,1,0:T(2,128)S(1)}, u32[]{:S(2)}, u32[]{:S(2)}) %collective-permute-start.5) | collective-permute-done | bytes 288 | tf_op jit(solution)/shard_map/ppermute | solution.py:123
  54.8 4.4 %collective-permute-done.6 = f32[2,2,16]{2,1,0:T(2,128)S(1)} collective-permute-done((f32[2,2,16]{2,1,0:T(2,128)S(1)}, f32[2,2,16]{2,1,0:T(2,128)S(1)}, u32[]{:S(2)}, u32[]{:S(2)}) %collective-permute-start.6) | collective-permute-done | bytes 288 | tf_op jit(solution)/shard_map/ppermute | solution.py:123
  59.3 0.0 copy-start.3
  59.3 0.9 %convolution_bitcast_fusion.1 = f32[2,2,16]{2,1,0:T(2,128)S(1)} fusion(f32[2,10,16]{2,1,0:T(8,128)S(1)} %concatenate.3, f32[8,16]{1,0:T(8,128)} %constant.16.clone, s32[]{:T(128)S(6)} %select_n.6, s32[]{:T(128)S(6)} %select_n.7), kind=kOutput, calls=%fused_computation.1 | convolution fusion | flops 7680 | bytes 2568 | tf_op jit(solution)/shard_map/yr,crx->cyx/dot_general | solution.py:169
  60.1 0.0 copy-done.3
  60.2 0.7 %convolution_bitcast_fusion = f32[2,1,2,16]{3,2,1,0:T(2,128)} fusion(f32[2,2,16]{2,1,0:T(2,128)S(1)} %convolution_bitcast_fusion.1, f32[16,16,1]{1,0,2:T(8,128)S(1)} %copy-done.3), kind=kOutput, calls=%fused_computation | convolution fusion | flops 12288 | bytes 1536 | tf_op jit(solution)/shard_map/cyr,xr->cyx/dot_general | solution.py:170
  (1 shorter events, 0.0 us)
Async XLA Ops:
  1.7 9.9 %collective-permute-start = (bf16[64,2048]{1,0:T(8,128)(2,1)S(1)}, bf16[64,2048]{1,0:T(8,128)(2,1)S(1)}, u32[]{:S(2)}, u32[]{:S(2)}) collective-permute-start(bf16[64,2048]{1,0:T(8,128)(2,1)S(1)} %get-tuple-element.7), channel_id=1, source_target_pairs={{0,1},{1,2},{2,3},{4,5},{5,6},{6,7},{8,9},{9,10},{10,11},{12,13},{... | collective-permute-start | bytes 786440 | tf_op jit(solution)/shard_map/ppermute | solution.py:123
  5.2 9.7 %collective-permute-start.1 = (bf16[64,2048]{1,0:T(8,128)(2,1)S(1)}, bf16[64,2048]{1,0:T(8,128)(2,1)S(1)}, u32[]{:S(2)}, u32[]{:S(2)}) collective-permute-start(bf16[64,2048]{1,0:T(8,128)(2,1)S(1)} %get-tuple-element.6), channel_id=1, source_target_pairs={{1,0},{2,1},{3,2},{5,4},{6,5},{7,6},{9,8},{10,9},{11,10},{13,12},{... | collective-permute-start | bytes 786440 | tf_op jit(solution)/shard_map/ppermute | solution.py:123
  11.6 3.2 %copy-start.1 = (bf16[64,2048]{1,0:T(8,128)(2,1)}, bf16[64,2048]{1,0:T(8,128)(2,1)S(1)}, u32[]{:S(2)}) copy-start(bf16[64,2048]{1,0:T(8,128)(2,1)S(1)} %collective-permute-done.above) | copy-start | bytes 786436
  14.9 0.7 %copy-start.2 = (bf16[64,2048]{1,0:T(8,128)(2,1)}, bf16[64,2048]{1,0:T(8,128)(2,1)S(1)}, u32[]{:S(2)}) copy-start(bf16[64,2048]{1,0:T(8,128)(2,1)S(1)} %collective-permute-done.1.below) | copy-start | bytes 786436
  15.6 5.7 %copy-start.4 = (s32[2,1,2,16]{3,2,1,0:T(2,128)S(1)}, s32[2,1,2,16]{3,2,1,0:T(2,128)}, u32[]{:S(2)}) copy-start(s32[2,1,2,16]{3,2,1,0:T(2,128)} %param.15) | copy-start | bytes 772
  19.4 16.3 %collective-permute-start.2 = (bf16[256,2048]{1,0:T(8,128)(2,1)}, bf16[256,2048]{1,0:T(8,128)(2,1)S(1)}, u32[]{:S(2)}, u32[]{:S(2)}) collective-permute-start(bf16[256,2048]{1,0:T(8,128)(2,1)} %shard_map.104.cur), channel_id=1, source_target_pairs={{0,4},{4,8},{8,12},{1,5},{5,9},{9,13},{2,6},{6,10},{10,14},{3,7},{... | collective-permute-start | bytes 3145736 | tf_op jit(solution)/shard_map/ppermute | solution.py:123
  35.7 1.0 %copy-start = (bf16[256,2048]{1,0:T(8,128)(2,1)}, bf16[256,2048]{1,0:T(8,128)(2,1)S(1)}, u32[]{:S(2)}) copy-start(bf16[256,2048]{1,0:T(8,128)(2,1)S(1)} %collective-permute-done.2.shifted) | copy-start | bytes 3145732
  44.5 9.6 %collective-permute-start.3 = (f32[2,2,16]{2,1,0:T(2,128)S(1)}, f32[2,2,16]{2,1,0:T(2,128)S(1)}, u32[]{:S(2)}, u32[]{:S(2)}) collective-permute-start(f32[2,2,16]{2,1,0:T(2,128)S(1)} %reshape_squeeze.3), channel_id=1, source_target_pairs={{0,2},{1,3},{4,6},{5,7},{8,10},{9,11},{12,14},{13,15},{16,18},{17,... | collective-permute-start | bytes 776 | tf_op jit(solution)/shard_map/ppermute | solution.py:123
  47.0 7.2 %collective-permute-start.4 = (f32[2,2,16]{2,1,0:T(2,128)S(1)}, f32[2,2,16]{2,1,0:T(2,128)S(1)}, u32[]{:S(2)}, u32[]{:S(2)}) collective-permute-start(f32[2,2,16]{2,1,0:T(2,128)S(1)} %reshape_squeeze.3), channel_id=1, source_target_pairs={{0,1},{1,2},{2,3},{4,5},{5,6},{6,7},{8,9},{9,10},{10,11},{12,13},{... | collective-permute-start | bytes 776 | tf_op jit(solution)/shard_map/ppermute | solution.py:123
  49.3 5.5 %collective-permute-start.5 = (f32[2,2,16]{2,1,0:T(2,128)S(1)}, f32[2,2,16]{2,1,0:T(2,128)S(1)}, u32[]{:S(2)}, u32[]{:S(2)}) collective-permute-start(f32[2,2,16]{2,1,0:T(2,128)S(1)} %reshape_squeeze.3), channel_id=1, source_target_pairs={{1,0},{2,1},{3,2},{5,4},{6,5},{7,6},{9,8},{10,9},{11,10},{13,12},{... | collective-permute-start | bytes 776 | tf_op jit(solution)/shard_map/ppermute | solution.py:123
  52.8 6.4 %collective-permute-start.6 = (f32[2,2,16]{2,1,0:T(2,128)S(1)}, f32[2,2,16]{2,1,0:T(2,128)S(1)}, u32[]{:S(2)}, u32[]{:S(2)}) collective-permute-start(f32[2,2,16]{2,1,0:T(2,128)S(1)} %reshape_squeeze.3), channel_id=1, source_target_pairs={{2,0},{3,1},{6,4},{7,5},{10,8},{11,9},{14,12},{15,13},{18,16},{19,... | collective-permute-start | bytes 776 | tf_op jit(solution)/shard_map/ppermute | solution.py:123
  59.3 0.9 %copy-start.3 = (f32[16,16,1]{1,0,2:T(8,128)S(1)}, f32[16,16,1]{1,0,2:T(8,128)}, u32[]{:S(2)}) copy-start(f32[16,16,1]{1,0,2:T(8,128)} %constant.24) | copy-start | bytes 3076
where the time goes:
time: 61.4 us; the launch traced here: 60.9 us
  waiting for transfers between devices  26.1 us (43%)
  starting transfers between devices  17.3 us (28%)
  Pallas kernels  10.7 us (17%)
  local copies, waits for them, and re-layouts  4.36 us (7%)
  matrix products  1.63 us (3%)
  between operations  0.74 us (1%)
    ppermute x7, waiting for transfers between devices, shift(): return lax.ppermute(x, axis, pairs)  26.1 us
    ppermute x7, starting transfers between devices, shift(): return lax.ppermute(x, axis, pairs)  17.3 us
    pallas_call x1, Pallas kernels, local(): pl.pallas_call(window_kernel, out_shape=jax.ShapeDtypeStruct((2, n_patche...  6.92 us
    pallas_call x1, Pallas kernels, local(): pl.pallas_call(functools.partial(render_kernel, n_rows * tiles), out_shap...  3.81 us
    unnamed x10, local copies, waits for them, and re-layouts  1.69 us
  transfers between devices with their start and end apart: 7, of which 5 were waited for; matrix products, arithmetic and copies ran while one was open for 1% of the time, Pallas kernels for 0%

commit v1 on v0

v1 whole, which is shorter than its diff:
```python
import functools

import jax
import jax.numpy as jnp
import numpy as np
from jax import lax
from jax.experimental import pallas as pl
from jax.experimental.pallas import tpu as pltpu
from jax.sharding import PartitionSpec as P

PATCH = 128
MARGIN = 64
SMOOTH_PASSES = 2
TAPS = (0.0625, 0.25, 0.375, 0.25, 0.0625)
BLOCK = 256
CHUNK = 512
WRAP = 16
MESH = pl.DeviceIdType.MESH


def smooth_operator(n):
    kernel = np.zeros((n, n))
    for k, tap in enumerate(TAPS):
        kernel += tap * np.eye(n, k=k - 2)
    kernel = kernel / kernel.sum(axis=1, keepdims=True)
    return np.linalg.matrix_power(kernel, SMOOTH_PASSES)


def tile_operators(tiles, patch_rows, patch_cols, hops):
    pad = hops * patch_rows
    rows = np.pad(smooth_operator(tiles * patch_rows), ((0, 0), (pad, pad)))
    cols = smooth_operator(patch_cols)
    ops = []
    for tile in range(tiles):
        at = tile * patch_rows
        ops.append(np.kron(rows[at : at + patch_rows, at : at + patch_rows + 2 * pad], cols))
    return np.stack(ops).astype(np.float32)


def two_tap(ids, first, weight):
    d = ids - first
    return jnp.where(d == 0, 1.0 - weight, jnp.where(d == 1, weight, 0.0)).astype(jnp.bfloat16)


def kernel(
    hops,
    sec, boundary, rshift, rfrac, cshift, cfrac, peak, ops,
    rendered, flow,
    stack, tabs, mix, cur, old, bpad, acc, peaks, field, op,
    local_sem, halo_send, halo_recv, mid_send, mid_recv, edge_send, edge_recv, flow_send, flow_recv,
):
    n_rows, n_cols = sec.shape[1:]
    n_px = n_cols // PATCH
    patch_rows = n_rows // PATCH
    chunks = n_cols // CHUNK
    tile, gz = lax.axis_index("ty"), lax.axis_index("gz")
    tiles, sections = lax.axis_size("ty"), lax.axis_size("gz")
    all_rows = n_rows * tiles

    def ty_ok(h):
        return jnp.logical_and(tile + h >= 0, tile + h < tiles)

    has_next, has_prev = gz + 1 < sections, gz > 0
    first = gz == 0
    ty_hops = [h for h in range(-hops, hops + 1) if h]
    peers = [({"ty": tile + h}, ty_ok(h)) for h in ty_hops]
    peers += [({"gz": gz + 1}, has_next), ({"gz": gz - 1}, has_prev)]

    load_sec = pltpu.make_async_copy(
        sec.at[0], stack.at[pl.ds(MARGIN, n_rows)], local_sem.at[0]
    )
    load_sec.start()
    load_op = pltpu.make_async_copy(ops.at[tile], op, local_sem.at[1])
    load_op.start()
    load_old = pltpu.make_async_copy(boundary, old, local_sem.at[2])

    @pl.when(first)
    def _():
        load_old.start()

    barrier = pltpu.get_barrier_semaphore()
    for where, ok in peers:
        @pl.when(ok)
        def _(where=where):
            pl.semaphore_signal(barrier, inc=1, device_id=where, device_id_type=MESH)
    pl.semaphore_wait(barrier, sum(jnp.where(ok, 1, 0) for _, ok in peers))

    down = pltpu.make_async_remote_copy(
        src_ref=sec.at[0, pl.ds(n_rows - MARGIN, MARGIN)],
        dst_ref=stack.at[pl.ds(0, MARGIN)],
        send_sem=halo_send.at[0], recv_sem=halo_recv.at[0],
        device_id={"ty": tile + 1}, device_id_type=MESH,
    )
    up = pltpu.make_async_remote_copy(
        src_ref=sec.at[0, pl.ds(0, MARGIN)],
        dst_ref=stack.at[pl.ds(MARGIN + n_rows, MARGIN)],
        send_sem=halo_send.at[1], recv_sem=halo_recv.at[1],
        device_id={"ty": tile - 1}, device_id_type=MESH,
    )

    @pl.when(ty_ok(1))
    def _():
        down.start()

    @pl.when(ty_ok(-1))
    def _():
        up.start()

    @pl.when(jnp.logical_not(ty_ok(-1)))
    def _():
        stack[0:MARGIN] = jnp.zeros((MARGIN, n_cols), jnp.bfloat16)

    @pl.when(jnp.logical_not(ty_ok(1)))
    def _():
        stack[MARGIN + n_rows :] = jnp.zeros((MARGIN, n_cols), jnp.bfloat16)

    for h in ty_hops:
        @pl.when(jnp.logical_not(ty_ok(h)))
        def _(h=h):
            field[h + hops] = jnp.zeros(field.shape[1:], jnp.float32)

    spans = []
    for b, x0 in enumerate(range(0, n_cols, BLOCK)):
        lo, hi = max(x0 - PATCH, 0), min(x0 + BLOCK + PATCH, n_cols)
        spans.append((x0, lo, hi))
        x = x0 + lax.broadcasted_iota(jnp.int32, (1, BLOCK), 1)
        src = jnp.clip(x + cshift[:, x0 : x0 + BLOCK], 0, n_cols - 2) - lo
        weight = cfrac[:, x0 : x0 + BLOCK].astype(jnp.float32) / 256.0
        ids = lax.broadcasted_iota(jnp.int32, (hi - lo, BLOCK), 0)
        tabs[b, 0 : hi - lo, :] = two_tap(ids, src, weight)

    y = tile * n_rows + lax.broadcasted_iota(jnp.int32, (1, n_rows), 1)
    src_row = jnp.clip(y + rshift[...], 0, all_rows - 2) - (tile * n_rows - MARGIN)
    row_weight = rfrac[...].astype(jnp.float32) / 256.0

    def mix_rows(o0, o1):
        g0, g1 = o0 // PATCH * PATCH, -(-o1 // PATCH) * PATCH
        span = o1 - o0 + 2 * MARGIN
        ids = o0 + lax.broadcasted_iota(jnp.int32, (span, g1 - g0), 0)
        table = two_tap(ids, src_row[:, g0:g1], row_weight[:, g0:g1])
        full = lax.dot_general(
            table, stack[o0 : o0 + span], (((0,), (0,)), ((), ())),
            preferred_element_type=jnp.float32,
        )
        return full[o0 - g0 : o1 - g0].astype(jnp.bfloat16)

    load_sec.wait()
    m0, m1 = MARGIN, n_rows - MARGIN
    for at in range(m0, m1, PATCH):
        mix[at : at + PATCH] = mix_rows(at, at + PATCH)

    def next_copy(rows, cols, send, recv):
        return pltpu.make_async_remote_copy(
            src_ref=cur.at[rows, cols], dst_ref=old.at[rows, cols],
            send_sem=send, recv_sem=recv,
            device_id={"gz": gz + 1}, device_id_type=MESH,
        )

    mids, tops, bots = [], [], []
    for c in range(chunks):
        cols = pl.ds(c * CHUNK, CHUNK)
        mids.append(next_copy(pl.ds(m0, m1 - m0), cols, mid_send.at[c], mid_recv.at[c]))
        tops.append(next_copy(pl.ds(0, m0), cols, edge_send.at[0, c], edge_recv.at[0, c]))
        bots.append(next_copy(pl.ds(m1, n_rows - m1), cols, edge_send.at[1, c], edge_recv.at[1, c]))

    def start_next(copies):
        @pl.when(has_next)
        def _():
            for copy in copies:
                copy.start()

    per = CHUNK // BLOCK
    for b, (x0, lo, hi) in enumerate(spans):
        cur[m0:m1, x0 : x0 + BLOCK] = jnp.dot(
            mix[m0:m1, lo:hi], tabs[b, 0 : hi - lo, :], preferred_element_type=jnp.float32
        ).astype(jnp.bfloat16)
        if b % per == per - 1:
            start_next([mids[b // per]])

    @pl.when(ty_ok(-1))
    def _():
        down.wait_recv()

    @pl.when(ty_ok(1))
    def _():
        up.wait_recv()

    mix[0:m0] = mix_rows(0, m0)
    mix[m1:n_rows] = mix_rows(m1, n_rows)
    for b, (x0, lo, hi) in enumerate(spans):
        edges = jnp.concatenate([mix[0:m0, lo:hi], mix[m1:n_rows, lo:hi]], axis=0)
        edges = jnp.dot(
            edges, tabs[b, 0 : hi - lo, :], preferred_element_type=jnp.float32
        ).astype(jnp.bfloat16)
        cur[0:m0, x0 : x0 + BLOCK] = edges[0:m0]
        cur[m1:n_rows, x0 : x0 + BLOCK] = edges[m0:]
        if b % per == per - 1:
            start_next([tops[b // per], bots[b // per]])

    save = pltpu.make_async_copy(cur, rendered.at[0], local_sem.at[3])
    save.start()

    @pl.when(first)
    def _():
        load_old.wait()

    def column(j, carry):
        cols = pl.ds(pl.multiple_of(j * PATCH, PATCH), PATCH)
        for p in range(patch_rows):
            rows = slice(p * PATCH, (p + 1) * PATCH)
            py, px = peak[0, 0, p, j], peak[1, 0, p, j]
            b = old[rows, cols].astype(jnp.float32)
            b = pltpu.roll(b, (PATCH - px) % PATCH, 1)
            bpad[p, 0:WRAP] = b[PATCH - WRAP :]
            bpad[p, WRAP : WRAP + PATCH] = b
            bpad[p, WRAP + PATCH :] = b[:WRAP]
            sums = [None] * 9
            for r in range(0, PATCH, 16):
                a = cur[p * PATCH + r : p * PATCH + r + 16, cols].astype(jnp.float32)
                a3 = (pltpu.roll(a, PATCH - 1, 1), a, pltpu.roll(a, 1, 1))
                for dy in range(3):
                    bb = bpad[p, pl.ds(WRAP - 1 + dy + r + py, 16), :]
                    for dx in range(3):
                        t = a3[dx] * bb
                        t = t[0:8] + t[8:16]
                        k = dy * 3 + dx
                        sums[k] = t if sums[k] is None else sums[k] + t
            at = pl.ds(p * n_px + j, 1)
            for k in range(9):
                acc[k, at, :] = jnp.sum(sums[k], axis=0, keepdims=True)
            peaks[0, at, :] = jnp.full((1, PATCH), py, jnp.int32).astype(jnp.float32)
            peaks[1, at, :] = jnp.full((1, PATCH), px, jnp.int32).astype(jnp.float32)
        return carry

    for c in range(chunks):
        @pl.when(has_prev)
        def _(c=c):
            mids[c].wait_recv()
            tops[c].wait_recv()
            bots[c].wait_recv()

        lax.fori_loop(c * CHUNK // PATCH, (c + 1) * CHUNK // PATCH, column, 0)

    w = [jnp.maximum(jnp.sum(acc[k], axis=-1, keepdims=True) / PATCH, 0.0) for k in range(9)]
    total = jnp.maximum(functools.reduce(lambda p, q: p + q, w), 1.0)
    row = ((w[6] + w[7] + w[8]) - (w[0] + w[1] + w[2])) / total
    col = ((w[2] + w[5] + w[8]) - (w[0] + w[3] + w[6])) / total
    lane = lax.broadcasted_iota(jnp.int32, field.shape[1:], 1)
    field[hops] = jnp.where(
        lane == 0, peaks[0] + row, jnp.where(lane == 1, peaks[1] + col, 0.0)
    )
    flows = []
    for i, h in enumerate(ty_hops):
        flows.append(
            pltpu.make_async_remote_copy(
                src_ref=field.at[hops], dst_ref=field.at[hops - h],
                send_sem=flow_send.at[i], recv_sem=flow_recv.at[i],
                device_id={"ty": tile + h}, device_id_type=MESH,
            )
        )

        @pl.when(ty_ok(h))
        def _(i=i):
            flows[i].start()

    load_op.wait()
    for i, h in enumerate(ty_hops):
        @pl.when(ty_ok(-h))
        def _(i=i):
            flows[i].wait_recv()

    wide = field.shape[0] * field.shape[1]
    smooth = lax.dot_general(
        field[...].reshape(wide, PATCH), op[...], (((0,), (1,)), ((), ())),
        preferred_element_type=jnp.float32, precision=lax.Precision.HIGHEST,
    )
    for p in range(patch_rows):
        flow[:, 0, p, :] = smooth[0:2, p * n_px : (p + 1) * n_px]

    for i, h in enumerate(ty_hops):
        @pl.when(ty_ok(h))
        def _(i=i):
            flows[i].wait_send()

    @pl.when(ty_ok(1))
    def _():
        down.wait_send()

    @pl.when(ty_ok(-1))
    def _():
        up.wait_send()

    @pl.when(has_next)
    def _():
        for copy in mids + tops + bots:
            copy.wait_send()

    save.wait()


def local(sections, boundary, row_shift, row_frac, col_shift, col_frac, peak_shift):
    n_rows, n_cols = sections.shape[1:]
    tiles = lax.axis_size("ty")
    patch_rows, patch_cols = n_rows // PATCH, n_cols // PATCH
    n_patches = patch_rows * patch_cols
    hops = -(-2 * SMOOTH_PASSES // patch_rows)
    chunks = n_cols // CHUNK
    ops = jnp.asarray(tile_operators(tiles, patch_rows, patch_cols, hops))
    anywhere = pl.BlockSpec(memory_space=pl.ANY)
    vmem = pl.BlockSpec(memory_space=pltpu.VMEM)
    smem = pl.BlockSpec(memory_space=pltpu.SMEM)
    dma = pltpu.SemaphoreType.DMA
    return pl.pallas_call(
        functools.partial(kernel, hops),
        out_shape=(
            jax.ShapeDtypeStruct(sections.shape, jnp.bfloat16),
            jax.ShapeDtypeStruct(peak_shift.shape, jnp.float32),
        ),
        in_specs=[anywhere, anywhere, vmem, vmem, vmem, vmem, smem, anywhere],
        out_specs=(anywhere, vmem),
        scratch_shapes=[
            pltpu.VMEM((n_rows + 2 * MARGIN, n_cols), jnp.bfloat16),
            pltpu.VMEM((n_cols // BLOCK, BLOCK + 2 * PATCH, BLOCK), jnp.bfloat16),
            pltpu.VMEM((n_rows, n_cols), jnp.bfloat16),
            pltpu.VMEM((n_rows, n_cols), jnp.bfloat16),
            pltpu.VMEM((n_rows, n_cols), jnp.bfloat16),
            pltpu.VMEM((patch_rows, PATCH + 2 * WRAP, PATCH), jnp.float32),
            pltpu.VMEM((9, n_patches, PATCH), jnp.float32),
            pltpu.VMEM((2, n_patches, PATCH), jnp.float32),
            pltpu.VMEM((2 * hops + 1, n_patches, PATCH), jnp.float32),
            pltpu.VMEM(ops.shape[1:], jnp.float32),
            dma((4,)), dma((2,)), dma((2,)), dma((chunks,)), dma((chunks,)),
            dma((2, chunks)), dma((2, chunks)), dma((2 * hops,)), dma((2 * hops,)),
        ],
        compiler_params=pltpu.CompilerParams(collective_id=0, has_side_effects=True),
    )(sections, boundary, row_shift, row_frac, col_shift, col_frac, peak_shift, ops)


def solution(mesh):
    in_specs = (
        P(("parts", "gz"), "ty", None),
        P(("parts", "ty"), None),
        P(("parts", "gz"), "ty"),
        P(("parts", "gz"), "ty"),
        P(("parts", "gz"), None),
        P(("parts", "gz"), None),
        P(None, ("parts", "gz"), "ty", None),
    )
    out_specs = (P(("parts", "gz"), "ty", None), P(None, ("parts", "gz"), "ty", None))
    return jax.shard_map(local, mesh=mesh, in_specs=in_specs, out_specs=out_specs, check_vma=False)
```

time: 61.4 us -> 28.2 us (0.46)
  the two profiles are of different devices: /device:TPU:10 before, /device:TPU:2 now
where the time goes in v1:
time: 28.2 us; the launch traced here: 28 us
  Pallas kernels  24.5 us (87%)
  local copies, waits for them, and re-layouts  2.89 us (10%)
  between operations  0.65 us (2%)
    pallas_call x1, Pallas kernels, local(): pl.pallas_call(functools.partial(kernel, hops), out_shape=(jax.ShapeDtype...  24.5 us
    unnamed x4, local copies, waits for them, and re-layouts  2.89 us

profile of v1, /device:TPU:2, one launch (start us, length us, event | category | flops | bytes accessed | tf_op | source)
XLA Modules:
  0.0 28.0 jit_solution(1913679234847203672)
XLA Ops:
  0.6 24.5 %shard_map.95 = (bf16[1,256,2048]{2,1,0:T(8,128)(2,1)}, f32[2,1,2,16]{3,2,1,0:T(2,128)}) custom-call(bf16[1,256,2048]{2,1,0:T(8,128)(2,1)} %sec.1, bf16[256,2048]{1,0:T(8,128)(2,1)} %boundary.1, s32[1,256]{1,0:T(1,128)} %rshift.1, s32[1,256]{1,0:T(1,128)} %rfrac.1, s32[1,2048]{1,0:T(1,128)} %cshift.1, s32[1,2048]{1,0:T(1,128)} %cfrac.1, ...), custom_call_target="tpu_custom_call" | custom-call | tf_op jit(solution)/shard_map/pallas_call | solution.py:313
  25.1 0.0 copy-start
  25.2 2.3 %copy.12 = bf16[1,256,2048]{2,1,0:T(8,128)(2,1)} copy(bf16[1,256,2048]{2,1,0:T(8,128)(2,1)} %get-tuple-element.4) | data formatting | bytes 2097152
  27.5 0.0 copy-done
  27.5 0.6 %copy.13 = f32[2,1,2,16]{3,2,1,0:T(2,128)} copy(f32[2,1,2,16]{3,2,1,0:T(2,128)S(1)} %copy-done) | data formatting | bytes 512
Async XLA Ops:
  25.1 2.3 %copy-start = (f32[2,1,2,16]{3,2,1,0:T(2,128)S(1)}, f32[2,1,2,16]{3,2,1,0:T(2,128)}, u32[]{:S(2)}) copy-start(f32[2,1,2,16]{3,2,1,0:T(2,128)} %get-tuple-element.5) | copy-start | bytes 772

commit v2 on v1

--- a/solution.py
+++ b/solution.py
@@ -46,9 +46,10 @@
     hops,
     sec, boundary, rshift, rfrac, cshift, cfrac, peak, ops,
     rendered, flow,
-    stack, tabs, mix, cur, old, bpad, acc, peaks, field, op,
+    stack, tabs, mix, old, bpad, acc, peaks, field, op,
     local_sem, halo_send, halo_recv, mid_send, mid_recv, edge_send, edge_recv, flow_send, flow_recv,
 ):
+    cur = rendered.at[0]
     n_rows, n_cols = sec.shape[1:]
     n_px = n_cols // PATCH
     patch_rows = n_rows // PATCH
@@ -85,26 +86,34 @@
             pl.semaphore_signal(barrier, inc=1, device_id=where, device_id_type=MESH)
     pl.semaphore_wait(barrier, sum(jnp.where(ok, 1, 0) for _, ok in peers))
 
-    down = pltpu.make_async_remote_copy(
-        src_ref=sec.at[0, pl.ds(n_rows - MARGIN, MARGIN)],
-        dst_ref=stack.at[pl.ds(0, MARGIN)],
-        send_sem=halo_send.at[0], recv_sem=halo_recv.at[0],
-        device_id={"ty": tile + 1}, device_id_type=MESH,
-    )
-    up = pltpu.make_async_remote_copy(
-        src_ref=sec.at[0, pl.ds(0, MARGIN)],
-        dst_ref=stack.at[pl.ds(MARGIN + n_rows, MARGIN)],
-        send_sem=halo_send.at[1], recv_sem=halo_recv.at[1],
-        device_id={"ty": tile - 1}, device_id_type=MESH,
-    )
-
-    @pl.when(ty_ok(1))
-    def _():
-        down.start()
-
-    @pl.when(ty_ok(-1))
-    def _():
-        up.start()
+    ends = [min((c + 1) * CHUNK + PATCH, n_cols) for c in range(chunks)]
+    downs, ups = [], []
+    for c, (x0, x1) in enumerate(zip([0] + ends, ends)):
+        cols = pl.ds(x0, x1 - x0)
+        downs.append(
+            pltpu.make_async_remote_copy(
+                src_ref=sec.at[0, pl.ds(n_rows - MARGIN, MARGIN), cols],
+                dst_ref=stack.at[pl.ds(0, MARGIN), cols],
+                send_sem=halo_send.at[0, c], recv_sem=halo_recv.at[0, c],
+                device_id={"ty": tile + 1}, device_id_type=MESH,
+            )
+        )
+        ups.append(
+            pltpu.make_async_remote_copy(
+                src_ref=sec.at[0, pl.ds(0, MARGIN), cols],
+                dst_ref=stack.at[pl.ds(MARGIN + n_rows, MARGIN), cols],
+                send_sem=halo_send.at[1, c], recv_sem=halo_recv.at[1, c],
+                device_id={"ty": tile - 1}, device_id_type=MESH,
+            )
+        )
+    for c in range(chunks):
+        @pl.when(ty_ok(1))
+        def _(c=c):
+            downs[c].start()
+
+        @pl.when(ty_ok(-1))
+        def _(c=c):
+            ups[c].start()
 
     @pl.when(jnp.logical_not(ty_ok(-1)))
     def _():
@@ -133,21 +142,24 @@
     src_row = jnp.clip(y + rshift[...], 0, all_rows - 2) - (tile * n_rows - MARGIN)
     row_weight = rfrac[...].astype(jnp.float32) / 256.0
 
-    def mix_rows(o0, o1):
+    def row_table(o0, o1):
         g0, g1 = o0 // PATCH * PATCH, -(-o1 // PATCH) * PATCH
         span = o1 - o0 + 2 * MARGIN
         ids = o0 + lax.broadcasted_iota(jnp.int32, (span, g1 - g0), 0)
-        table = two_tap(ids, src_row[:, g0:g1], row_weight[:, g0:g1])
+        return two_tap(ids, src_row[:, g0:g1], row_weight[:, g0:g1])
+
+    def mix_rows(table, o0, o1, x0, x1):
+        g0 = o0 // PATCH * PATCH
         full = lax.dot_general(
-            table, stack[o0 : o0 + span], (((0,), (0,)), ((), ())),
+            table, stack[o0 : o1 + 2 * MARGIN, x0:x1], (((0,), (0,)), ((), ())),
             preferred_element_type=jnp.float32,
         )
-        return full[o0 - g0 : o1 - g0].astype(jnp.bfloat16)
+        mix[o0:o1, x0:x1] = full[o0 - g0 : o1 - g0].astype(jnp.bfloat16)
 
     load_sec.wait()
     m0, m1 = MARGIN, n_rows - MARGIN
     for at in range(m0, m1, PATCH):
-        mix[at : at + PATCH] = mix_rows(at, at + PATCH)
+        mix_rows(row_table(at, at + PATCH), at, at + PATCH, 0, n_cols)
 
     def next_copy(rows, cols, send, recv):
         return pltpu.make_async_remote_copy(
@@ -177,28 +189,29 @@
         if b % per == per - 1:
             start_next([mids[b // per]])
 
-    @pl.when(ty_ok(-1))
-    def _():
-        down.wait_recv()
-
-    @pl.when(ty_ok(1))
-    def _():
-        up.wait_recv()
-
-    mix[0:m0] = mix_rows(0, m0)
-    mix[m1:n_rows] = mix_rows(m1, n_rows)
-    for b, (x0, lo, hi) in enumerate(spans):
-        edges = jnp.concatenate([mix[0:m0, lo:hi], mix[m1:n_rows, lo:hi]], axis=0)
-        edges = jnp.dot(
-            edges, tabs[b, 0 : hi - lo, :], preferred_element_type=jnp.float32
-        ).astype(jnp.bfloat16)
-        cur[0:m0, x0 : x0 + BLOCK] = edges[0:m0]
-        cur[m1:n_rows, x0 : x0 + BLOCK] = edges[m0:]
-        if b % per == per - 1:
-            start_next([tops[b // per], bots[b // per]])
-
-    save = pltpu.make_async_copy(cur, rendered.at[0], local_sem.at[3])
-    save.start()
+    top_table, bot_table = row_table(0, m0), row_table(m1, n_rows)
+
+    def render_edges(c):
+        @pl.when(ty_ok(-1))
+        def _():
+            downs[c].wait_recv()
+
+        @pl.when(ty_ok(1))
+        def _():
+            ups[c].wait_recv()
+
+        x0, x1 = ([0] + ends)[c], ends[c]
+        mix_rows(top_table, 0, m0, x0, x1)
+        mix_rows(bot_table, m1, n_rows, x0, x1)
+        for b in range(c * per, (c + 1) * per):
+            x0, lo, hi = spans[b]
+            edges = jnp.concatenate([mix[0:m0, lo:hi], mix[m1:n_rows, lo:hi]], axis=0)
+            edges = jnp.dot(
+                edges, tabs[b, 0 : hi - lo, :], preferred_element_type=jnp.float32
+            ).astype(jnp.bfloat16)
+            cur[0:m0, x0 : x0 + BLOCK] = edges[0:m0]
+            cur[m1:n_rows, x0 : x0 + BLOCK] = edges[m0:]
+        start_next([tops[c], bots[c]])
 
     @pl.when(first)
     def _():
@@ -232,7 +245,13 @@
             peaks[1, at, :] = jnp.full((1, PATCH), px, jnp.int32).astype(jnp.float32)
         return carry
 
-    for c in range(chunks):
+    for step in range(chunks + 1):
+        if step < chunks:
+            render_edges(step)
+        c = step - 1
+        if c < 0:
+            continue
+
         @pl.when(has_prev)
         def _(c=c):
             mids[c].wait_recv()
@@ -284,18 +303,18 @@
 
     @pl.when(ty_ok(1))
     def _():
-        down.wait_send()
+        for copy in downs:
+            copy.wait_send()
 
     @pl.when(ty_ok(-1))
     def _():
-        up.wait_send()
+        for copy in ups:
+            copy.wait_send()
 
     @pl.when(has_next)
     def _():
         for copy in mids + tops + bots:
             copy.wait_send()
-
-    save.wait()
 
 
 def local(sections, boundary, row_shift, row_frac, col_shift, col_frac, peak_shift):
@@ -313,15 +332,14 @@
     return pl.pallas_call(
         functools.partial(kernel, hops),
         out_shape=(
-            jax.ShapeDtypeStruct(sections.shape, jnp.bfloat16),
-            jax.ShapeDtypeStruct(peak_shift.shape, jnp.float32),
+            pltpu.VMEM(sections.shape, jnp.bfloat16),
+            pltpu.VMEM(peak_shift.shape, jnp.float32),
         ),
         in_specs=[anywhere, anywhere, vmem, vmem, vmem, vmem, smem, anywhere],
-        out_specs=(anywhere, vmem),
+        out_specs=(vmem, vmem),
         scratch_shapes=[
             pltpu.VMEM((n_rows + 2 * MARGIN, n_cols), jnp.bfloat16),
             pltpu.VMEM((n_cols // BLOCK, BLOCK + 2 * PATCH, BLOCK), jnp.bfloat16),
-            pltpu.VMEM((n_rows, n_cols), jnp.bfloat16),
             pltpu.VMEM((n_rows, n_cols), jnp.bfloat16),
             pltpu.VMEM((n_rows, n_cols), jnp.bfloat16),
             pltpu.VMEM((patch_rows, PATCH + 2 * WRAP, PATCH), jnp.float32),
@@ -329,7 +347,7 @@
             pltpu.VMEM((2, n_patches, PATCH), jnp.float32),
             pltpu.VMEM((2 * hops + 1, n_patches, PATCH), jnp.float32),
             pltpu.VMEM(ops.shape[1:], jnp.float32),
-            dma((4,)), dma((2,)), dma((2,)), dma((chunks,)), dma((chunks,)),
+            dma((3,)), dma((2, chunks)), dma((2, chunks)), dma((chunks,)), dma((chunks,)),
             dma((2, chunks)), dma((2, chunks)), dma((2 * hops,)), dma((2 * hops,)),
         ],
         compiler_params=pltpu.CompilerParams(collective_id=0, has_side_effects=True),

time: 28.2 us -> 25.3 us (0.90)
  Pallas kernels: 24.5 us -> 22.9 us
  local copies, waits for them, and re-layouts: 2.89 us -> 1.55 us
    pallas_call x1, Pallas kernels: 24.5 us -> 22.9 us  [local(): pl.pallas_call(functools.partial(kernel, hops), out_shape=(pltpu.VMEM(sec...]
    unnamed x4 -> x2, local copies, waits for them, and re-layouts: 2.89 us -> 1.55 us
where the time goes in v2:
time: 25.3 us; the launch traced here: 25.1 us
  Pallas kernels  22.9 us (91%)
  local copies, waits for them, and re-layouts  1.55 us (6%)
  between operations  0.64 us (3%)
    pallas_call x1, Pallas kernels, local(): pl.pallas_call(functools.partial(kernel, hops), out_shape=(pltpu.VMEM(sec...  22.9 us
    unnamed x2, local copies, waits for them, and re-layouts  1.55 us

profile of v2, /device:TPU:2, one launch (start us, length us, event | category | flops | bytes accessed | tf_op | source)
XLA Modules:
  0.0 25.1 jit_solution(18158757114453281)
XLA Ops:
  0.6 22.9 %shard_map.95 = (bf16[1,256,2048]{2,1,0:T(8,128)(2,1)S(1)}, f32[2,1,2,16]{3,2,1,0:T(2,128)S(1)}) custom-call(bf16[1,256,2048]{2,1,0:T(8,128)(2,1)} %sec.1, bf16[256,2048]{1,0:T(8,128)(2,1)} %boundary.1, s32[1,256]{1,0:T(1,128)} %rshift.1, s32[1,256]{1,0:T(1,128)} %rfrac.1, s32[1,2048]{1,0:T(1,128)} %cshift.1, s32[1,2048]{1,0:T(1,128)} %cfrac.1, ...), custom_call_target="tpu_custom_call" | custom-call | tf_op jit(solution)/shard_map/pallas_call | solution.py:332
  23.6 1.0 %copy.12 = bf16[1,256,2048]{2,1,0:T(8,128)(2,1)} copy(bf16[1,256,2048]{2,1,0:T(8,128)(2,1)S(1)} %get-tuple-element.2) | data formatting | bytes 2097152
  24.6 0.6 %copy.13 = f32[2,1,2,16]{3,2,1,0:T(2,128)} copy(f32[2,1,2,16]{3,2,1,0:T(2,128)S(1)} %get-tuple-element.3) | data formatting | bytes 512

commit v3 on v2

--- a/solution.py
+++ b/solution.py
@@ -84,6 +84,26 @@
         @pl.when(ok)
         def _(where=where):
             pl.semaphore_signal(barrier, inc=1, device_id=where, device_id_type=MESH)
+    spans = []
+    for x0 in range(0, n_cols, BLOCK):
+        spans.append((x0, max(x0 - PATCH, 0), min(x0 + BLOCK + PATCH, n_cols)))
+
+    def col_table(b):
+        x0, lo, hi = spans[b]
+        x = x0 + lax.broadcasted_iota(jnp.int32, (1, BLOCK), 1)
+        src = jnp.clip(x + cshift[:, x0 : x0 + BLOCK], 0, n_cols - 2) - lo
+        weight = cfrac[:, x0 : x0 + BLOCK].astype(jnp.float32) / 256.0
+        ids = lax.broadcasted_iota(jnp.int32, (hi - lo, BLOCK), 0)
+        tabs[b, 0 : hi - lo, :] = two_tap(ids, src, weight)
+
+    per = CHUNK // BLOCK
+    for b in range(2 * per):
+        col_table(b)
+
+    y = tile * n_rows + lax.broadcasted_iota(jnp.int32, (1, n_rows), 1)
+    src_row = jnp.clip(y + rshift[...], 0, all_rows - 2) - (tile * n_rows - MARGIN)
+    row_weight = rfrac[...].astype(jnp.float32) / 256.0
+
     pl.semaphore_wait(barrier, sum(jnp.where(ok, 1, 0) for _, ok in peers))
 
     ends = [min((c + 1) * CHUNK + PATCH, n_cols) for c in range(chunks)]
@@ -128,20 +148,6 @@
         def _(h=h):
             field[h + hops] = jnp.zeros(field.shape[1:], jnp.float32)
 
-    spans = []
-    for b, x0 in enumerate(range(0, n_cols, BLOCK)):
-        lo, hi = max(x0 - PATCH, 0), min(x0 + BLOCK + PATCH, n_cols)
-        spans.append((x0, lo, hi))
-        x = x0 + lax.broadcasted_iota(jnp.int32, (1, BLOCK), 1)
-        src = jnp.clip(x + cshift[:, x0 : x0 + BLOCK], 0, n_cols - 2) - lo
-        weight = cfrac[:, x0 : x0 + BLOCK].astype(jnp.float32) / 256.0
-        ids = lax.broadcasted_iota(jnp.int32, (hi - lo, BLOCK), 0)
-        tabs[b, 0 : hi - lo, :] = two_tap(ids, src, weight)
-
-    y = tile * n_rows + lax.broadcasted_iota(jnp.int32, (1, n_rows), 1)
-    src_row = jnp.clip(y + rshift[...], 0, all_rows - 2) - (tile * n_rows - MARGIN)
-    row_weight = rfrac[...].astype(jnp.float32) / 256.0
-
     def row_table(o0, o1):
         g0, g1 = o0 // PATCH * PATCH, -(-o1 // PATCH) * PATCH
         span = o1 - o0 + 2 * MARGIN
@@ -158,8 +164,7 @@
 
     load_sec.wait()
     m0, m1 = MARGIN, n_rows - MARGIN
-    for at in range(m0, m1, PATCH):
-        mix_rows(row_table(at, at + PATCH), at, at + PATCH, 0, n_cols)
+    mid_tables = [(at, row_table(at, at + PATCH)) for at in range(m0, m1, PATCH)]
 
     def next_copy(rows, cols, send, recv):
         return pltpu.make_async_remote_copy(
@@ -181,13 +186,18 @@
             for copy in copies:
                 copy.start()
 
-    per = CHUNK // BLOCK
-    for b, (x0, lo, hi) in enumerate(spans):
-        cur[m0:m1, x0 : x0 + BLOCK] = jnp.dot(
-            mix[m0:m1, lo:hi], tabs[b, 0 : hi - lo, :], preferred_element_type=jnp.float32
-        ).astype(jnp.bfloat16)
-        if b % per == per - 1:
-            start_next([mids[b // per]])
+    for c in range(chunks):
+        x0, x1 = ([0] + ends)[c], ends[c]
+        for at, table in mid_tables:
+            mix_rows(table, at, at + PATCH, x0, x1)
+        for b in range(c * per, (c + 1) * per):
+            if b >= 2 * per:
+                col_table(b)
+            x0, lo, hi = spans[b]
+            cur[m0:m1, x0 : x0 + BLOCK] = jnp.dot(
+                mix[m0:m1, lo:hi], tabs[b, 0 : hi - lo, :], preferred_element_type=jnp.float32
+            ).astype(jnp.bfloat16)
+        start_next([mids[c]])
 
     top_table, bot_table = row_table(0, m0), row_table(m1, n_rows)
 
@@ -317,6 +327,14 @@
             copy.wait_send()
 
 
+def write_kernel(a, b, out_a, out_b, sem):
+    copies = [pltpu.make_async_copy(a, out_a, sem.at[0]), pltpu.make_async_copy(b, out_b, sem.at[1])]
+    for copy in copies:
+        copy.start()
+    for copy in copies:
+        copy.wait()
+
+
 def local(sections, boundary, row_shift, row_frac, col_shift, col_frac, peak_shift):
     n_rows, n_cols = sections.shape[1:]
     tiles = lax.axis_size("ty")
@@ -329,7 +347,7 @@
     vmem = pl.BlockSpec(memory_space=pltpu.VMEM)
     smem = pl.BlockSpec(memory_space=pltpu.SMEM)
     dma = pltpu.SemaphoreType.DMA
-    return pl.pallas_call(
+    held = pl.pallas_call(
         functools.partial(kernel, hops),
         out_shape=(
             pltpu.VMEM(sections.shape, jnp.bfloat16),
@@ -352,6 +370,16 @@
         ],
         compiler_params=pltpu.CompilerParams(collective_id=0, has_side_effects=True),
     )(sections, boundary, row_shift, row_frac, col_shift, col_frac, peak_shift, ops)
+    return pl.pallas_call(
+        write_kernel,
+        out_shape=(
+            jax.ShapeDtypeStruct(sections.shape, jnp.bfloat16),
+            jax.ShapeDtypeStruct(peak_shift.shape, jnp.float32),
+        ),
+        in_specs=[vmem, vmem],
+        out_specs=(anywhere, anywhere),
+        scratch_shapes=[dma((2,))],
+    )(*[pltpu.with_memory_space_constraint(x, pltpu.VMEM) for x in held])
 
 
 def solution(mesh):

time: 25.3 us -> 23.8 us (0.941)
  local copies, waits for them, and re-layouts: 1.55 us -> 0 us
    unnamed x2 -> x0, local copies, waits for them, and re-layouts: 1.55 us -> none
    pallas_call x0 -> x1, Pallas kernels: none -> 0.99 us  [local(): pl.pallas_call(write_kernel, out_shape=(jax.ShapeDtypeStruct(sections.sha...]
    pallas_call x1, Pallas kernels: 22.9 us -> 22 us  [local(): pl.pallas_call(functools.partial(kernel, hops), out_shape=(pltpu.VMEM(sec...]
where the time goes in v3:
time: 23.8 us; the launch traced here: 23.6 us
  Pallas kernels  23 us (97%)
  between operations  0.64 us (3%)
    pallas_call x1, Pallas kernels, local(): pl.pallas_call(functools.partial(kernel, hops), out_shape=(pltpu.VMEM(sec...  22 us
    pallas_call x1, Pallas kernels, local(): pl.pallas_call(write_kernel, out_shape=(jax.ShapeDtypeStruct(sections.sha...  0.99 us

profile of v3, /device:TPU:2, one launch (start us, length us, event | category | flops | bytes accessed | tf_op | source)
XLA Modules:
  0.0 23.6 jit_solution(8042030056667191868)
XLA Ops:
  0.6 22.0 %shard_map.95 = (bf16[1,256,2048]{2,1,0:T(8,128)(2,1)S(1)}, f32[2,1,2,16]{3,2,1,0:T(2,128)S(1)}) custom-call(bf16[1,256,2048]{2,1,0:T(8,128)(2,1)} %sec.1, bf16[256,2048]{1,0:T(8,128)(2,1)} %boundary.1, s32[1,256]{1,0:T(1,128)} %rshift.1, s32[1,256]{1,0:T(1,128)} %rfrac.1, s32[1,2048]{1,0:T(1,128)} %cshift.1, s32[1,2048]{1,0:T(1,128)} %cfrac.1, ...), custom_call_target="tpu_custom_call" | custom-call | tf_op jit(solution)/shard_map/pallas_call | solution.py:350
  22.6 1.0 %shard_map.96 = (bf16[1,256,2048]{2,1,0:T(8,128)(2,1)}, f32[2,1,2,16]{3,2,1,0:T(2,128)}) custom-call(bf16[1,256,2048]{2,1,0:T(8,128)(2,1)S(1)} %get-tuple-element.4.a, f32[2,1,2,16]{3,2,1,0:T(2,128)S(1)} %get-tuple-element.5.b), custom_call_target="tpu_custom_call" | custom-call | tf_op jit(solution)/shard_map/pallas_call | solution.py:373

commit v4 on v3

--- a/solution.py
+++ b/solution.py
@@ -13,7 +13,8 @@
 SMOOTH_PASSES = 2
 TAPS = (0.0625, 0.25, 0.375, 0.25, 0.0625)
 BLOCK = 256
-CHUNK = 512
+CHUNK = 256
+EARLY = 4
 WRAP = 16
 MESH = pl.DeviceIdType.MESH
 
@@ -64,7 +65,7 @@
     has_next, has_prev = gz + 1 < sections, gz > 0
     first = gz == 0
     ty_hops = [h for h in range(-hops, hops + 1) if h]
-    peers = [({"ty": tile + h}, ty_ok(h)) for h in ty_hops]
+    peers = [({"ty": tile + h}, ty_ok(h)) for h in ty_hops if abs(h) != 2]
     peers += [({"gz": gz + 1}, has_next), ({"gz": gz - 1}, has_prev)]
 
     load_sec = pltpu.make_async_copy(
@@ -97,7 +98,7 @@
         tabs[b, 0 : hi - lo, :] = two_tap(ids, src, weight)
 
     per = CHUNK // BLOCK
-    for b in range(2 * per):
+    for b in range(min(EARLY, len(spans))):
         col_table(b)
 
     y = tile * n_rows + lax.broadcasted_iota(jnp.int32, (1, n_rows), 1)
@@ -191,7 +192,7 @@
         for at, table in mid_tables:
             mix_rows(table, at, at + PATCH, x0, x1)
         for b in range(c * per, (c + 1) * per):
-            if b >= 2 * per:
+            if b >= EARLY:
                 col_table(b)
             x0, lo, hi = spans[b]
             cur[m0:m1, x0 : x0 + BLOCK] = jnp.dot(

time: 23.8 us -> 23.9 us (level); the launches traced: 23.6 us -> 23.4 us
  no operation moved by 1% of the time
where the time goes in v4:
time: 23.9 us; the launch traced here: 23.4 us
  Pallas kernels  22.8 us (95%)
  between operations  0.64 us (3%)
    pallas_call x1, Pallas kernels, local(): pl.pallas_call(functools.partial(kernel, hops), out_shape=(pltpu.VMEM(sec...  21.8 us
    pallas_call x1, Pallas kernels, local(): pl.pallas_call(write_kernel, out_shape=(jax.ShapeDtypeStruct(sections.sha...  0.99 us

profile of v4, /device:TPU:2, one launch (start us, length us, event | category | flops | bytes accessed | tf_op | source)
XLA Modules:
  0.0 23.4 jit_solution(8898265748228615161)
XLA Ops:
  0.6 21.8 %shard_map.95 = (bf16[1,256,2048]{2,1,0:T(8,128)(2,1)S(1)}, f32[2,1,2,16]{3,2,1,0:T(2,128)S(1)}) custom-call(bf16[1,256,2048]{2,1,0:T(8,128)(2,1)} %sec.1, bf16[256,2048]{1,0:T(8,128)(2,1)} %boundary.1, s32[1,256]{1,0:T(1,128)} %rshift.1, s32[1,256]{1,0:T(1,128)} %rfrac.1, s32[1,2048]{1,0:T(1,128)} %cshift.1, s32[1,2048]{1,0:T(1,128)} %cfrac.1, ...), custom_call_target="tpu_custom_call" | custom-call | tf_op jit(solution)/shard_map/pallas_call | solution.py:351
  22.4 1.0 %shard_map.96 = (bf16[1,256,2048]{2,1,0:T(8,128)(2,1)}, f32[2,1,2,16]{3,2,1,0:T(2,128)}) custom-call(bf16[1,256,2048]{2,1,0:T(8,128)(2,1)S(1)} %get-tuple-element.4.a, f32[2,1,2,16]{3,2,1,0:T(2,128)S(1)} %get-tuple-element.5.b), custom_call_target="tpu_custom_call" | custom-call | tf_op jit(solution)/shard_map/pallas_call | solution.py:374
